TPU v7x, 256 devices: a whole 4x4x8 slice. The times are simulated.
256 devices in a mesh: batch: 128 (over y, z, x), tile: 2 (over core).
Axes of the slice: x: 4, y: 4, z: 8, core: 2. Of those that a mesh axis runs over, the one named last changes fastest.
Arguments:
- first_view: bfloat16 [256, 8192], P('batch'), may hold values from -1500 to 1500
- second_view: bfloat16 [256, 8192], P('batch'), may hold values from -1500 to 1500
Outputs:
- grad_first: bfloat16 [256, 8192], P('batch', 'tile')
- grad_second: bfloat16 [256, 8192], P('batch', 'tile')
All inputs are finite; a program needn't handle non-finite values.
Results may differ from a plain program's by a relative error of at most 0.0043.
Values may be sent and summed in bfloat16 or wider, within the bound.
A program may use at most 64 MiB of HBM per device.

v0:
```python
import jax
import jax.numpy as jnp
from jax import lax
from jax.sharding import PartitionSpec as P

BAND = 16
epsilon = 1e-05
decorrelation = 0.0051


def fold_rows(received, row_count, row_groups, group_size, block_width):
    return (
        received.reshape(row_count, row_groups, group_size, block_width)
        .sum(2)
        .reshape(row_count, row_groups * block_width)
    )


def fold_cols(received, row_count, row_groups, group_size, block_width):
    return (
        received.reshape(row_count, row_groups, group_size, block_width)
        .sum(1)
        .reshape(row_count, group_size * block_width)
    )


def per_device(first_view, second_view):
    row_count, feature_width = first_view.shape
    device_count = lax.axis_size("batch")
    band_index = lax.axis_index("batch")
    tile_index = lax.axis_index("tile")
    total_rows = row_count * device_count
    half_width = feature_width // 2
    first_float = first_view.astype(jnp.float32)
    second_float = second_view.astype(jnp.float32)
    moments = lax.psum(
        (
            jnp.sum(first_float, 0),
            jnp.sum(first_float * first_float, 0),
            jnp.sum(second_float, 0),
            jnp.sum(second_float * second_float, 0),
        ),
        "batch",
    )
    mean_first = moments[0] / total_rows
    inverse_first = lax.rsqrt(moments[1] / total_rows - mean_first * mean_first + epsilon)
    mean_second = moments[2] / total_rows
    inverse_second = lax.rsqrt(moments[3] / total_rows - mean_second * mean_second + epsilon)
    norm_first = ((first_float - mean_first) * inverse_first).astype(jnp.bfloat16)
    norm_second = ((second_float - mean_second) * inverse_second).astype(jnp.bfloat16)
    group_size = BAND
    row_groups = device_count // group_size
    block_rows = feature_width * group_size // device_count
    block_cols = feature_width // (2 * group_size)
    row_band = band_index // group_size
    column_block = band_index % group_size + group_size * tile_index
    send_first = jnp.broadcast_to(
        norm_first.reshape(row_count, row_groups, 1, block_rows),
        (row_count, row_groups, group_size, block_rows),
    ).reshape(row_count, device_count * block_rows)
    picked = lax.dynamic_slice_in_dim(
        norm_second.reshape(row_count, 2, group_size, block_cols), tile_index, 1, 1
    )
    send_second = jnp.broadcast_to(picked, (row_count, row_groups, group_size, block_cols)).reshape(
        row_count, device_count * block_cols
    )
    whole_first, whole_second = (
        lax.all_to_all(send_first, "batch", split_axis=1, concat_axis=0, tiled=True),
        lax.all_to_all(send_second, "batch", split_axis=1, concat_axis=0, tiled=True),
    )
    correlation = (
        lax.dot_general(
            whole_first, whole_second, (((0,), (0,)), ((), ())), preferred_element_type=jnp.float32
        )
        / total_rows
    )
    row_ids = row_band * block_rows + lax.iota(jnp.int32, block_rows)
    col_ids = column_block * block_cols + lax.iota(jnp.int32, block_cols)
    on_diagonal = row_ids[:, None] == col_ids[None, :]
    slope_tile = jnp.where(on_diagonal, correlation - 1.0, decorrelation * correlation).astype(
        jnp.bfloat16
    )
    pull_first = lax.dot_general(
        whole_second, slope_tile, (((1,), (1,)), ((), ())), preferred_element_type=jnp.float32
    )
    pull_second = jnp.dot(whole_first, slope_tile, preferred_element_type=jnp.float32)
    half_start = tile_index * half_width
    norm_first_half = lax.dynamic_slice_in_dim(norm_first, half_start, half_width, 1).astype(
        jnp.float32
    )
    norm_second_half = lax.dynamic_slice_in_dim(norm_second, half_start, half_width, 1).astype(
        jnp.float32
    )
    inverse_first_half = lax.dynamic_slice_in_dim(inverse_first, half_start, half_width, 0)
    inverse_second_half = lax.dynamic_slice_in_dim(inverse_second, half_start, half_width, 0)
    back_first, back_second = (
        lax.all_to_all(pull_first, "batch", split_axis=0, concat_axis=1, tiled=True),
        lax.all_to_all(pull_second, "batch", split_axis=0, concat_axis=1, tiled=True),
    )
    full_first = fold_rows(back_first, row_count, row_groups, group_size, block_rows)
    pull_second_half = fold_cols(back_second, row_count, row_groups, group_size, block_cols)
    pull_first_half = lax.psum_scatter(full_first, "tile", scatter_dimension=1, tiled=True)
    column_sums = lax.psum(
        (
            jnp.sum(pull_first_half * norm_first_half, 0, keepdims=True),
            jnp.sum(pull_second_half * norm_second_half, 0, keepdims=True),
        ),
        "batch",
    )
    stat_first = column_sums[0] / total_rows
    stat_second = column_sums[1] / total_rows
    grad_first = (inverse_first_half * (pull_first_half - norm_first_half * stat_first)).astype(
        jnp.bfloat16
    )
    grad_second = (
        inverse_second_half * (pull_second_half - norm_second_half * stat_second)
    ).astype(jnp.bfloat16)
    return (grad_first, grad_second)


def solution(mesh):
    return jax.shard_map(
        per_device,
        mesh=mesh,
        in_specs=(P("batch", None), P("batch", None)),
        out_specs=(P("batch", "tile"), P("batch", "tile")),
        check_vma=False,
    )
```

profile of v0, /device:TPU:0, one launch (start us, length us, event | category | flops | bytes accessed | tf_op | source)
XLA Modules:
  0.0 1036.5 jit_solution(13418832312192321948)
XLA Ops:
  7.2 1.5 convert_reduce_fusion.1
  8.7 1.5 convert_reduce_fusion
  10.3 217.0 %all-reduce.4.cloned.1.call-done = (f32[8192]{0:T(1024)}, f32[8192]{0:T(1024)}, f32[8192]{0:T(1024)}, f32[8192]{0:T(1024)}) async-done(((f32[8192]{0:T(1024)}, f32[8192]{0:T(1024)}, f32[8192]{0:T(1024)}, f32[8192]{0:T(1024)}), (f32[8192]{0:T(1024)}, f32[8192]{0:T(1024)}, f32[8192]{0:T(1024)}, f32[8192]{0:T(1024)})) %all-reduce.4.cloned.1.call-update) | async-done | bytes 131088 | tf_op jit(solution)/shard_map/psum | solution.py:36
  227.3 0.8 broadcast_multiply_fusion
  228.1 0.8 fusion.11
  228.9 0.1 broadcast_in_dim.15
  229.0 1.3 copy.30
  230.3 10.2 all-to-all-start.1
  240.6 0.8 fusion.13
  241.4 14.9 %all-to-all-done.1 = bf16[2,128,1024]{2,0,1:T(2,128)(2,1)S(1)} async-done(((bf16[2,128,1024]{2,0,1:T(2,128)(2,1)}), bf16[2,128,1024]{2,0,1:T(2,128)(2,1)S(1)}, u32[]{:S(2)}, u32[]{:S(2)}) %all-to-all-start.1) | async-done | bytes 524320 | tf_op jit(solution)/shard_map/all_to_all | solution.py:68
  256.3 0.7 broadcast_in_dim.13
  257.1 6.3 all-to-all-start
  263.4 0.5 copy.31
  264.0 11.5 %all-to-all-done = bf16[2,128,256]{2,0,1:T(2,128)(2,1)S(1)} async-done(((bf16[2,128,256]{2,0,1:T(2,128)(2,1)}), bf16[2,128,256]{2,0,1:T(2,128)(2,1)S(1)}, u32[]{:S(2)}, u32[]{:S(2)}) %all-to-all-start) | async-done | bytes 131104 | tf_op jit(solution)/shard_map/all_to_all | solution.py:69
  275.4 0.4 fusion
  275.8 0.3 fusion.4
  276.2 1.8 copy.32
  278.0 6.2 all-to-all-start.2
  284.1 0.3 fusion.1
  284.5 0.9 copy.34
  285.4 22.4 %all-to-all-done.2 = f32[128,2,1024]{2,1,0:T(2,128)S(1)} async-done(((f32[128,2,1024]{2,1,0:T(2,128)}), f32[128,2,1024]{2,1,0:T(2,128)S(1)}, u32[]{:S(2)}, u32[]{:S(2)}) %all-to-all-start.2) | async-done | bytes 1048608 | tf_op jit(solution)/shard_map/all_to_all | solution.py:97
  307.9 7.0 all-to-all-start.3
  314.9 0.2 bitcast_reduce_fusion
  315.1 2.6 copy.38
  317.8 10.1 all-to-all-done.3
  327.9 0.1 reduce_sum.78
  328.1 9.0 reduce-scatter.4.cloned.1.call-done
  337.0 2.2 copy.39
  339.2 0.1 fusion.15
  339.3 689.0 %all-reduce = (f32[1,4096]{1,0:T(1,128)S(1)}, f32[1,4096]{1,0:T(1,128)S(1)}) all-reduce(f32[1,4096]{1,0:T(1,128)S(1)} %bitcast.62, f32[1,4096]{1,0:T(1,128)S(1)} %bitcast.60), channel_id=1, replica_groups=mesh['batch'=128,'tile'=2] {'batch'}, use_global_device_ids=true, to_apply=%region_11.12 | all-reduce | flops 8192 | bytes 65536 | tf_op jit(solution)/shard_map/psum | solution.py:103
  1028.3 0.6 fusion.18
  1029.0 0.6 fusion.22
  (15 shorter events, 0.3 us)
Async XLA Ops:
  7.2 220.1 %all-reduce.4.cloned.1.call-start = ((), (), s32[]{:S(2)}) async-start(), calls=%async_computation.6 | async-start | bytes 262144 | tf_op jit(solution)/shard_map/psum | solution.py:36
  230.3 26.0 %all-to-all-start.1 = ((bf16[2,128,1024]{2,0,1:T(2,128)(2,1)}), bf16[2,128,1024]{2,0,1:T(2,128)(2,1)S(1)}, u32[]{:S(2)}, u32[]{:S(2)}) async-start(bf16[2,128,1024]{2,0,1:T(2,128)(2,1)} %copy.30), calls=%async_computation.1 | async-start | bytes 1048576 | tf_op jit(solution)/shard_map/all_to_all | solution.py:68
  257.1 18.4 %all-to-all-start = ((bf16[2,128,256]{2,0,1:T(2,128)(2,1)}), bf16[2,128,256]{2,0,1:T(2,128)(2,1)S(1)}, u32[]{:S(2)}, u32[]{:S(2)}) async-start(bf16[2,128,256]{2,0,1:T(2,128)(2,1)} %bitcast.1), calls=%async_computation | async-start | bytes 262144 | tf_op jit(solution)/shard_map/all_to_all | solution.py:69
  278.0 29.9 %all-to-all-start.2 = ((f32[128,2,1024]{2,1,0:T(2,128)}), f32[128,2,1024]{2,1,0:T(2,128)S(1)}, u32[]{:S(2)}, u32[]{:S(2)}) async-start(f32[128,2,1024]{2,1,0:T(2,128)} %copy.32), calls=%async_computation.2 | async-start | bytes 2097152 | tf_op jit(solution)/shard_map/all_to_all | solution.py:97
  307.9 20.1 %all-to-all-start.3 = ((f32[128,2,256]{2,1,0:T(2,128)}), f32[128,2,256]{2,1,0:T(2,128)S(1)}, u32[]{:S(2)}, u32[]{:S(2)}) async-start(f32[128,2,256]{2,1,0:T(2,128)} %copy.34), calls=%async_computation.3 | async-start | bytes 524288 | tf_op jit(solution)/shard_map/all_to_all | solution.py:98
  314.8 22.2 %reduce-scatter.4.cloned.1.call-start = ((), (), s32[]{:S(2)}) async-start(), calls=%async_computation.5 | async-start | bytes 6291456
Sparse Core Ops, SparseCore 0:
  13.7 213.4 all-reduce.3
  318.4 18.5 reduce-scatter.3
where the time goes:
time: 1040 us
  blocking collectives  689 us (66%)
  waiting for transfers between devices  285 us (27%)
  starting transfers between devices  29.8 us (3%)
  between operations  14.3 us (1%)
    psum x1, blocking collectives, per_device(): lax.psum((jnp.sum(pull_first_half * norm_first_half, 0, keepdims=True), j...  689 us
    psum x1, waiting for transfers between devices, per_device(): lax.psum((jnp.sum(first_float, 0), jnp.sum(first_float * first_float, 0),...  217 us
    all_to_all x1, waiting for transfers between devices, per_device(): lax.all_to_all(pull_first, 'batch', split_axis=0, concat_axis=1, tiled=True)  22.4 us
  transfers between devices with their start and end apart: 6, of which 6 were waited for; matrix products, arithmetic and copies ran while one was open for 1% of the time, Pallas kernels for 0%

commit v1 on v0

--- a/solution.py
+++ b/solution.py
@@ -65,7 +65,12 @@
         row_count, device_count * block_cols
     )
     whole_first, whole_second = (
-        lax.all_to_all(send_first, "batch", split_axis=1, concat_axis=0, tiled=True),
+        jnp.concatenate(
+            lax.all_to_all(
+                jnp.stack(jnp.split(send_first, lax.axis_size("batch"), axis=1)), "batch", 0, 0
+            ),
+            axis=0,
+        ),
         lax.all_to_all(send_second, "batch", split_axis=1, concat_axis=0, tiled=True),
     )
     correlation = (

time: 1040 us -> 1110 us (1.067)
  local copies, waits for them, and re-layouts: 10.2 us -> 85 us
    unnamed x4 -> x132, local copies, waits for them, and re-layouts: 4.84 us -> 80.8 us
    all_to_all x1, waiting for transfers between devices: 11.5 us -> 0.01 us  [per_device(): lax.all_to_all(send_second, 'batch', split_axis=1, concat_axis=0, tiled=T...]
  transfers between devices with their start and end apart: 6 -> 6, of which waited for: 6 -> 5; matrix products, arithmetic and copies ran while one was open for 1% -> 7% of each run, Pallas kernels for 0% -> 0%
where the time goes in v1:
time: 1110 us
  blocking collectives  689 us (62%)
  waiting for transfers between devices  274 us (25%)
  local copies, waits for them, and re-layouts  85 us (8%)
  starting transfers between devices  37.8 us (3%)
  between operations  14.3 us (1%)
    psum x1, blocking collectives, per_device(): lax.psum((jnp.sum(pull_first_half * norm_first_half, 0, keepdims=True), j...  689 us
    psum x1, waiting for transfers between devices, per_device(): lax.psum((jnp.sum(first_float, 0), jnp.sum(first_float * first_float, 0),...  217 us
    unnamed x132, local copies, waits for them, and re-layouts  80.8 us
    all_to_all x1, waiting for transfers between devices, per_device(): lax.all_to_all(pull_first, 'batch', split_axis=0, concat_axis=1, tiled=True)  23 us
  transfers between devices with their start and end apart: 6, of which 5 were waited for; matrix products, arithmetic and copies ran while one was open for 7% of the time, Pallas kernels for 0%

profile of v1, /device:TPU:0, one launch (start us, length us, event | category | flops | bytes accessed | tf_op | source)
XLA Modules:
  0.0 1108.8 jit_solution(10157285211499366384)
XLA Ops:
  7.2 1.5 convert_reduce_fusion.1
  8.7 1.5 convert_reduce_fusion
  10.3 217.0 %all-reduce.4.cloned.1.call-done = (f32[8192]{0:T(1024)}, f32[8192]{0:T(1024)}, f32[8192]{0:T(1024)}, f32[8192]{0:T(1024)}) async-done(((f32[8192]{0:T(1024)}, f32[8192]{0:T(1024)}, f32[8192]{0:T(1024)}, f32[8192]{0:T(1024)}), (f32[8192]{0:T(1024)}, f32[8192]{0:T(1024)}, f32[8192]{0:T(1024)}, f32[8192]{0:T(1024)})) %all-reduce.4.cloned.1.call-update) | async-done | bytes 131088 | tf_op jit(solution)/shard_map/psum | solution.py:36
  227.3 0.8 broadcast_multiply_fusion
  228.1 0.8 fusion.11
  228.9 0.8 fusion.13
  229.8 0.8 copy.4101
  230.6 10.2 all-to-all-start
  245.0 0.6 constant_dynamic-update-slice_fusion.121
  247.4 0.6 constant_dynamic-update-slice_fusion.117
  253.9 0.6 constant_dynamic-update-slice_fusion.106
  262.8 0.6 constant_dynamic-update-slice_fusion.91
  281.9 0.6 constant_dynamic-update-slice_fusion.59
  288.4 0.6 constant_dynamic-update-slice_fusion.48
  292.0 0.6 constant_dynamic-update-slice_fusion.42
  300.3 0.6 constant_dynamic-update-slice_fusion.28
  305.7 0.6 constant_dynamic-update-slice_fusion.19
  309.9 0.6 constant_dynamic-update-slice_fusion.12
  317.6 13.8 %all-to-all-start.1 = ((bf16[128,2,1024]{2,1,0:T(2,128)(2,1)}), bf16[128,2,1024]{2,1,0:T(2,128)(2,1)S(1)}, u32[]{:S(2)}, u32[]{:S(2)}) async-start(bf16[128,2,1024]{2,1,0:T(2,128)(2,1)} %constant_dynamic-update-slice_fusion), calls=%async_computation.1 | async-start | bytes 1048576 | tf_op jit(solution)/shard_map/all_to_all | solution.py:69
  331.4 15.3 %all-to-all-done.1 = bf16[128,2,1024]{2,1,0:T(2,128)(2,1)S(1)} async-done(((bf16[128,2,1024]{2,1,0:T(2,128)(2,1)}), bf16[128,2,1024]{2,1,0:T(2,128)(2,1)S(1)}, u32[]{:S(2)}, u32[]{:S(2)}) %all-to-all-start.1) | async-done | bytes 524320 | tf_op jit(solution)/shard_map/all_to_all | solution.py:69
  347.4 1.8 copy.4104
  349.2 6.7 all-to-all-start.2
  356.3 0.9 copy.4107
  357.2 23.0 %all-to-all-done.2 = f32[128,2,1024]{2,1,0:T(2,128)S(1)} async-done(((f32[128,2,1024]{2,1,0:T(2,128)}), f32[128,2,1024]{2,1,0:T(2,128)S(1)}, u32[]{:S(2)}, u32[]{:S(2)}) %all-to-all-start.2) | async-done | bytes 1048608 | tf_op jit(solution)/shard_map/all_to_all | solution.py:102
  380.2 7.0 all-to-all-start.3
  387.4 2.6 copy.4111
  390.1 10.1 all-to-all-done.3
  400.4 9.0 reduce-scatter.4.cloned.1.call-done
  409.3 2.2 copy.4112
  411.6 689.0 %all-reduce = (f32[1,4096]{1,0:T(1,128)S(1)}, f32[1,4096]{1,0:T(1,128)S(1)}) all-reduce(f32[1,4096]{1,0:T(1,128)S(1)} %bitcast.702, f32[1,4096]{1,0:T(1,128)S(1)} %bitcast.700), channel_id=1, replica_groups=mesh['batch'=128,'tile'=2] {'batch'}, use_global_device_ids=true, to_apply=%region_11.12 | all-reduce | flops 8192 | bytes 65536 | tf_op jit(solution)/shard_map/psum | solution.py:108
  1100.7 0.6 fusion.18
  1101.3 0.6 fusion.22
  (142 shorter events, 72.4 us)
Async XLA Ops:
  7.2 220.1 %all-reduce.4.cloned.1.call-start = ((), (), s32[]{:S(2)}) async-start(), calls=%async_computation.6 | async-start | bytes 262144 | tf_op jit(solution)/shard_map/psum | solution.py:36
  230.6 87.0 %all-to-all-start = ((bf16[2,128,256]{2,0,1:T(2,128)(2,1)}), bf16[2,128,256]{2,0,1:T(2,128)(2,1)S(1)}, u32[]{:S(2)}, u32[]{:S(2)}) async-start(bf16[2,128,256]{2,0,1:T(2,128)(2,1)} %copy.4101), calls=%async_computation | async-start | bytes 262144 | tf_op jit(solution)/shard_map/all_to_all | solution.py:74
  317.6 29.1 %all-to-all-start.1 = ((bf16[128,2,1024]{2,1,0:T(2,128)(2,1)}), bf16[128,2,1024]{2,1,0:T(2,128)(2,1)S(1)}, u32[]{:S(2)}, u32[]{:S(2)}) async-start(bf16[128,2,1024]{2,1,0:T(2,128)(2,1)} %constant_dynamic-update-slice_fusion), calls=%async_computation.1 | async-start | bytes 1048576 | tf_op jit(solution)/shard_map/all_to_all | solution.py:69
  349.2 30.9 %all-to-all-start.2 = ((f32[128,2,1024]{2,1,0:T(2,128)}), f32[128,2,1024]{2,1,0:T(2,128)S(1)}, u32[]{:S(2)}, u32[]{:S(2)}) async-start(f32[128,2,1024]{2,1,0:T(2,128)} %copy.4104), calls=%async_computation.2 | async-start | bytes 2097152 | tf_op jit(solution)/shard_map/all_to_all | solution.py:102
  380.2 20.1 %all-to-all-start.3 = ((f32[128,2,256]{2,1,0:T(2,128)}), f32[128,2,256]{2,1,0:T(2,128)S(1)}, u32[]{:S(2)}, u32[]{:S(2)}) async-start(f32[128,2,256]{2,1,0:T(2,128)} %copy.4107), calls=%async_computation.3 | async-start | bytes 524288 | tf_op jit(solution)/shard_map/all_to_all | solution.py:103
  387.2 22.2 %reduce-scatter.4.cloned.1.call-start = ((), (), s32[]{:S(2)}) async-start(), calls=%async_computation.5 | async-start | bytes 6291456
Sparse Core Ops, SparseCore 0:
  13.7 213.4 all-reduce.3
  390.7 18.5 reduce-scatter.3
